TPU v7x, 256 devices: a whole 4x4x8 slice. The times are simulated.
256 devices in a mesh: rows: 16 (over z, core), feat: 16 (over x, y).
Axes of the slice: x: 4, y: 4, z: 8, core: 2. Of those that a mesh axis runs over, the one named last changes fastest.
Arguments:
- features: bfloat16 [16384, 16384], P('rows', 'feat'), may hold values from -0.046875 to 0.046875
- inverse_gram: float32 [16384, 1024], P('feat'), as said below
- targets: float32 [128, 16384], P('feat', 'rows'), may hold values from -6 to 6
Outputs:
- weights: float32 [128, 16384], P(None, 'feat')
- residual: float32 [128, 16384], P('feat', 'rows')
Inputs may be any that keep to these rules, and one draw needn't show every extreme that they name: Each block of inverse_gram is symmetric.
All inputs are finite; a program needn't handle non-finite values.
Results may differ from a plain program's by a relative error of at most 0.007.
Values sent between devices are 32-bit elements; how exact they have to be, the bound alone decides.
No kernel may reach another device: no remote copies, remote signals or barrier semaphores. Data moves between devices by JAX's collectives and lax.ppermute only.
A program may use at most 64 MiB of HBM per device.

v0:
```python
import jax
import jax.numpy as jnp
from jax import lax
from jax.sharding import PartitionSpec as P

TGT = 128
TURNS = 2
ridge_weight = 0.5


def passed_along(block, axis, distance):
    devices = range(lax.axis_size(axis))
    route = [((i - distance) % len(devices), i) for i in devices]
    return lax.ppermute(block, axis, route)


def local(features, inverse_gram, targets):
    block_count = lax.axis_size("feat")
    position = lax.axis_index("feat")
    panel_width = targets.shape[0]

    def refine(panel_rows, panel_weights):
        partial_value = jnp.dot(
            panel_rows.astype(jnp.bfloat16), features, preferred_element_type=jnp.float32
        )
        projection = lax.psum(partial_value, "rows")
        increment = jnp.dot(
            projection - ridge_weight * panel_weights, inverse_gram, precision=lax.Precision.HIGHEST
        )
        fitted = lax.dot_general(
            increment.astype(jnp.bfloat16),
            features,
            (((1,), (1,)), ((), ())),
            preferred_element_type=jnp.float32,
        )
        return (panel_rows - fitted, panel_weights + increment)

    def advance(section, carried):
        residual, weights = carried
        panel_index = (position - section) % block_count
        start = panel_index * panel_width
        panel_weights = lax.dynamic_slice_in_dim(weights, start, panel_width, 0)
        residual, panel_weights = refine(residual, panel_weights)
        weights = lax.dynamic_update_slice_in_dim(weights, panel_weights, start, 0)
        residual = passed_along(residual, "feat", 1)
        return (residual, weights)

    carried = (targets, jnp.zeros((TGT, features.shape[1]), jnp.float32))
    for sweep_index in range(TURNS):
        offset = sweep_index * block_count

        def sweep_step(inner, state, offset=offset):
            return advance(inner + offset, state)

        carried = lax.fori_loop(0, block_count, sweep_step, carried)
    residual, weights = carried
    return (weights, residual)


def solution(mesh):
    placed = (P("rows", "feat"), P("feat", None), P("feat", "rows"))
    return jax.shard_map(
        local,
        mesh=mesh,
        in_specs=placed,
        out_specs=(P(None, "feat"), P("feat", "rows")),
        check_vma=False,
    )
```

profile of v0, /device:TPU:0, one launch (start us, length us, event | category | flops | bytes accessed | tf_op | source)
XLA Modules:
  0.0 1925.4 jit_solution(16532286769631520528)
XLA Ops:
  1.4 963.3 %while.34 = (s32[]{:T(128)}, f32[8,1024]{1,0:T(8,128)S(1)}, f32[128,1024]{1,0:T(8,128)S(1)}, bf16[1024,1024]{1,0:T(8,128)(2,1)}, s32[]{:T(128)}, /*index=5*/f32[...) while((s32[]{:T(128)}, f32[8,1024]{1,0:T(8,128)S(1)}, ...), condition=%wide.region_2.3_spmd, body=%wide.region_0.2_spmd.sunk | while | flops 134275072 | bytes 17334632 | solution.py:55
  3.4 49.1 %psum.30 = f32[8,1024]{1,0:T(8,128)S(1)} all-reduce(f32[8,1024]{1,0:T(8,128)S(1)} %fusion.48), channel_id=1, replica_groups=mesh['rows'=16,'feat'=16] {'rows'}, use_global_device_ids=true, to_apply=%region_1.1 | all-reduce | flops 8192 | bytes 65536 | tf_op jit(solution)/shard_map/while/body/eval_jaxpr/psum | solution.py:26
  66.9 45.7 %psum.30 = f32[8,1024]{1,0:T(8,128)S(1)} all-reduce(f32[8,1024]{1,0:T(8,128)S(1)} %fusion.48), channel_id=1, replica_groups=mesh['rows'=16,'feat'=16] {'rows'}, use_global_device_ids=true, to_apply=%region_1.1 | all-reduce | flops 8192 | bytes 65536 | tf_op jit(solution)/shard_map/while/body/eval_jaxpr/psum | solution.py:26
  126.9 45.7 %psum.30 = f32[8,1024]{1,0:T(8,128)S(1)} all-reduce(f32[8,1024]{1,0:T(8,128)S(1)} %fusion.48), channel_id=1, replica_groups=mesh['rows'=16,'feat'=16] {'rows'}, use_global_device_ids=true, to_apply=%region_1.1 | all-reduce | flops 8192 | bytes 65536 | tf_op jit(solution)/shard_map/while/body/eval_jaxpr/psum | solution.py:26
  186.9 45.7 %psum.30 = f32[8,1024]{1,0:T(8,128)S(1)} all-reduce(f32[8,1024]{1,0:T(8,128)S(1)} %fusion.48), channel_id=1, replica_groups=mesh['rows'=16,'feat'=16] {'rows'}, use_global_device_ids=true, to_apply=%region_1.1 | all-reduce | flops 8192 | bytes 65536 | tf_op jit(solution)/shard_map/while/body/eval_jaxpr/psum | solution.py:26
  246.9 45.7 %psum.30 = f32[8,1024]{1,0:T(8,128)S(1)} all-reduce(f32[8,1024]{1,0:T(8,128)S(1)} %fusion.48), channel_id=1, replica_groups=mesh['rows'=16,'feat'=16] {'rows'}, use_global_device_ids=true, to_apply=%region_1.1 | all-reduce | flops 8192 | bytes 65536 | tf_op jit(solution)/shard_map/while/body/eval_jaxpr/psum | solution.py:26
  306.8 45.7 %psum.30 = f32[8,1024]{1,0:T(8,128)S(1)} all-reduce(f32[8,1024]{1,0:T(8,128)S(1)} %fusion.48), channel_id=1, replica_groups=mesh['rows'=16,'feat'=16] {'rows'}, use_global_device_ids=true, to_apply=%region_1.1 | all-reduce | flops 8192 | bytes 65536 | tf_op jit(solution)/shard_map/while/body/eval_jaxpr/psum | solution.py:26
  366.8 45.7 %psum.30 = f32[8,1024]{1,0:T(8,128)S(1)} all-reduce(f32[8,1024]{1,0:T(8,128)S(1)} %fusion.48), channel_id=1, replica_groups=mesh['rows'=16,'feat'=16] {'rows'}, use_global_device_ids=true, to_apply=%region_1.1 | all-reduce | flops 8192 | bytes 65536 | tf_op jit(solution)/shard_map/while/body/eval_jaxpr/psum | solution.py:26
  426.8 45.7 %psum.30 = f32[8,1024]{1,0:T(8,128)S(1)} all-reduce(f32[8,1024]{1,0:T(8,128)S(1)} %fusion.48), channel_id=1, replica_groups=mesh['rows'=16,'feat'=16] {'rows'}, use_global_device_ids=true, to_apply=%region_1.1 | all-reduce | flops 8192 | bytes 65536 | tf_op jit(solution)/shard_map/while/body/eval_jaxpr/psum | solution.py:26
  486.8 45.7 %psum.30 = f32[8,1024]{1,0:T(8,128)S(1)} all-reduce(f32[8,1024]{1,0:T(8,128)S(1)} %fusion.48), channel_id=1, replica_groups=mesh['rows'=16,'feat'=16] {'rows'}, use_global_device_ids=true, to_apply=%region_1.1 | all-reduce | flops 8192 | bytes 65536 | tf_op jit(solution)/shard_map/while/body/eval_jaxpr/psum | solution.py:26
  606.8 45.7 %psum.30 = f32[8,1024]{1,0:T(8,128)S(1)} all-reduce(f32[8,1024]{1,0:T(8,128)S(1)} %fusion.48), channel_id=1, replica_groups=mesh['rows'=16,'feat'=16] {'rows'}, use_global_device_ids=true, to_apply=%region_1.1 | all-reduce | flops 8192 | bytes 65536 | tf_op jit(solution)/shard_map/while/body/eval_jaxpr/psum | solution.py:26
  666.8 45.7 %psum.30 = f32[8,1024]{1,0:T(8,128)S(1)} all-reduce(f32[8,1024]{1,0:T(8,128)S(1)} %fusion.48), channel_id=1, replica_groups=mesh['rows'=16,'feat'=16] {'rows'}, use_global_device_ids=true, to_apply=%region_1.1 | all-reduce | flops 8192 | bytes 65536 | tf_op jit(solution)/shard_map/while/body/eval_jaxpr/psum | solution.py:26
  786.8 45.7 %psum.30 = f32[8,1024]{1,0:T(8,128)S(1)} all-reduce(f32[8,1024]{1,0:T(8,128)S(1)} %fusion.48), channel_id=1, replica_groups=mesh['rows'=16,'feat'=16] {'rows'}, use_global_device_ids=true, to_apply=%region_1.1 | all-reduce | flops 8192 | bytes 65536 | tf_op jit(solution)/shard_map/while/body/eval_jaxpr/psum | solution.py:26
  846.7 45.7 %psum.30 = f32[8,1024]{1,0:T(8,128)S(1)} all-reduce(f32[8,1024]{1,0:T(8,128)S(1)} %fusion.48), channel_id=1, replica_groups=mesh['rows'=16,'feat'=16] {'rows'}, use_global_device_ids=true, to_apply=%region_1.1 | all-reduce | flops 8192 | bytes 65536 | tf_op jit(solution)/shard_map/while/body/eval_jaxpr/psum | solution.py:26
  964.8 959.8 %while.35 = (s32[]{:T(128)}, f32[8,1024]{1,0:T(8,128)S(1)}, f32[128,1024]{1,0:T(8,128)S(1)}, bf16[1024,1024]{1,0:T(8,128)(2,1)}, s32[]{:T(128)}, /*index=5*/f32[...) while((s32[]{:T(128)}, f32[8,1024]{1,0:T(8,128)S(1)}, ...), condition=%wide.region_5.6_spmd, body=%wide.region_3.5_spmd.sunk | while | flops 134275072 | bytes 17334644 | solution.py:55
  966.7 45.7 %psum.31 = f32[8,1024]{1,0:T(8,128)S(1)} all-reduce(f32[8,1024]{1,0:T(8,128)S(1)} %fusion.56), channel_id=1, replica_groups=mesh['rows'=16,'feat'=16] {'rows'}, use_global_device_ids=true, to_apply=%region_4.4 | all-reduce | flops 8192 | bytes 65536 | tf_op jit(solution)/shard_map/while/body/eval_jaxpr/psum | solution.py:26
  1086.7 45.7 %psum.31 = f32[8,1024]{1,0:T(8,128)S(1)} all-reduce(f32[8,1024]{1,0:T(8,128)S(1)} %fusion.56), channel_id=1, replica_groups=mesh['rows'=16,'feat'=16] {'rows'}, use_global_device_ids=true, to_apply=%region_4.4 | all-reduce | flops 8192 | bytes 65536 | tf_op jit(solution)/shard_map/while/body/eval_jaxpr/psum | solution.py:26
  1146.7 45.7 %psum.31 = f32[8,1024]{1,0:T(8,128)S(1)} all-reduce(f32[8,1024]{1,0:T(8,128)S(1)} %fusion.56), channel_id=1, replica_groups=mesh['rows'=16,'feat'=16] {'rows'}, use_global_device_ids=true, to_apply=%region_4.4 | all-reduce | flops 8192 | bytes 65536 | tf_op jit(solution)/shard_map/while/body/eval_jaxpr/psum | solution.py:26
  1266.7 45.7 %psum.31 = f32[8,1024]{1,0:T(8,128)S(1)} all-reduce(f32[8,1024]{1,0:T(8,128)S(1)} %fusion.56), channel_id=1, replica_groups=mesh['rows'=16,'feat'=16] {'rows'}, use_global_device_ids=true, to_apply=%region_4.4 | all-reduce | flops 8192 | bytes 65536 | tf_op jit(solution)/shard_map/while/body/eval_jaxpr/psum | solution.py:26
  1326.7 45.7 %psum.31 = f32[8,1024]{1,0:T(8,128)S(1)} all-reduce(f32[8,1024]{1,0:T(8,128)S(1)} %fusion.56), channel_id=1, replica_groups=mesh['rows'=16,'feat'=16] {'rows'}, use_global_device_ids=true, to_apply=%region_4.4 | all-reduce | flops 8192 | bytes 65536 | tf_op jit(solution)/shard_map/while/body/eval_jaxpr/psum | solution.py:26
  1446.6 45.7 %psum.31 = f32[8,1024]{1,0:T(8,128)S(1)} all-reduce(f32[8,1024]{1,0:T(8,128)S(1)} %fusion.56), channel_id=1, replica_groups=mesh['rows'=16,'feat'=16] {'rows'}, use_global_device_ids=true, to_apply=%region_4.4 | all-reduce | flops 8192 | bytes 65536 | tf_op jit(solution)/shard_map/while/body/eval_jaxpr/psum | solution.py:26
  1506.6 45.7 %psum.31 = f32[8,1024]{1,0:T(8,128)S(1)} all-reduce(f32[8,1024]{1,0:T(8,128)S(1)} %fusion.56), channel_id=1, replica_groups=mesh['rows'=16,'feat'=16] {'rows'}, use_global_device_ids=true, to_apply=%region_4.4 | all-reduce | flops 8192 | bytes 65536 | tf_op jit(solution)/shard_map/while/body/eval_jaxpr/psum | solution.py:26
  1686.6 45.7 %psum.31 = f32[8,1024]{1,0:T(8,128)S(1)} all-reduce(f32[8,1024]{1,0:T(8,128)S(1)} %fusion.56), channel_id=1, replica_groups=mesh['rows'=16,'feat'=16] {'rows'}, use_global_device_ids=true, to_apply=%region_4.4 | all-reduce | flops 8192 | bytes 65536 | tf_op jit(solution)/shard_map/while/body/eval_jaxpr/psum | solution.py:26
  1866.6 45.7 %psum.31 = f32[8,1024]{1,0:T(8,128)S(1)} all-reduce(f32[8,1024]{1,0:T(8,128)S(1)} %fusion.56), channel_id=1, replica_groups=mesh['rows'=16,'feat'=16] {'rows'}, use_global_device_ids=true, to_apply=%region_4.4 | all-reduce | flops 8192 | bytes 65536 | tf_op jit(solution)/shard_map/while/body/eval_jaxpr/psum | solution.py:26
  (271 shorter events, 915.3 us)
Async XLA Ops:
  57.7 7.3 collective-permute-start
  117.7 7.3 collective-permute-start
  177.6 7.3 collective-permute-start
  237.6 7.3 collective-permute-start
  297.6 7.3 collective-permute-start
  357.6 7.3 collective-permute-start
  417.6 7.3 collective-permute-start
  477.6 7.3 collective-permute-start
  537.6 7.3 collective-permute-start
  597.6 7.3 collective-permute-start
  657.6 7.3 collective-permute-start
  717.5 7.3 collective-permute-start
  777.5 7.3 collective-permute-start
  837.5 7.3 collective-permute-start
  897.5 7.3 collective-permute-start
  957.5 7.3 collective-permute-start
  1017.5 7.3 collective-permute-start.1
  1077.5 7.3 collective-permute-start.1
  1137.5 7.3 collective-permute-start.1
  1197.5 7.3 collective-permute-start.1
  1317.4 7.3 collective-permute-start.1
  1497.4 7.3 collective-permute-start.1
  1677.4 7.3 collective-permute-start.1
  1857.3 7.3 collective-permute-start.1
  (41 other events, 200.2 us)
where the time goes:
time: 1930 us
  blocking collectives  1470 us (76%)
  waiting for transfers between devices  229 us (12%)
  matrix products  225 us (12%)
    psum x32, blocking collectives, refine(): projection = lax.psum(partial_value, 'rows')  1470 us
    ppermute x32, waiting for transfers between devices, passed_along(): return lax.ppermute(block, axis, route)  229 us
    dot_general x32, matrix products, refine(): jnp.dot(projection - ridge_weight * panel_weights, inverse_gram, precisio...  141 us
    dot_general x32, matrix products, refine(): jnp.dot(panel_rows.astype(jnp.bfloat16), features, preferred_element_type...  63.1 us
  transfers between devices with their start and end apart: 32, of which 32 were waited for; matrix products, arithmetic and copies ran while one was open for 0% of the time, Pallas kernels for 0%

commit v1 on v0

--- a/solution.py
+++ b/solution.py
@@ -23,7 +23,7 @@
         partial_value = jnp.dot(
             panel_rows.astype(jnp.bfloat16), features, preferred_element_type=jnp.float32
         )
-        projection = lax.psum(partial_value, "rows")
+        projection = jnp.sum(lax.all_gather(partial_value, "rows"), axis=0)
         increment = jnp.dot(
             projection - ridge_weight * panel_weights, inverse_gram, precision=lax.Precision.HIGHEST
         )

time: 1930 us -> 996 us (0.52)
  blocking collectives: 1470 us -> 532 us
    psum x32 -> x0, blocking collectives: 1470 us -> none  [refine(): projection = lax.psum(partial_value, 'rows')]
    all_gather x0 -> x32, blocking collectives: none -> 532 us  [refine(): projection = jnp.sum(lax.all_gather(partial_value, 'rows'), axis=0)]
where the time goes in v1:
time: 996 us; the launch traced here: 993 us
  blocking collectives  532 us (53%)
  waiting for transfers between devices  229 us (23%)
  matrix products  225 us (23%)
    all_gather x32, blocking collectives, refine(): projection = jnp.sum(lax.all_gather(partial_value, 'rows'), axis=0)  532 us
    ppermute x32, waiting for transfers between devices, passed_along(): return lax.ppermute(block, axis, route)  229 us
    dot_general x32, matrix products, refine(): jnp.dot(projection - ridge_weight * panel_weights, inverse_gram, precisio...  141 us
    dot_general x32, matrix products, refine(): jnp.dot(panel_rows.astype(jnp.bfloat16), features, preferred_element_type...  63.1 us
    dot_general x32, matrix products, refine(): lax.dot_general(increment.astype(jnp.bfloat16), features, (((1,), (1,)),...  20.6 us
  transfers between devices with their start and end apart: 32, of which 32 were waited for; matrix products, arithmetic and copies ran while one was open for 0% of the time, Pallas kernels for 0%

profile of v1, /device:TPU:0, one launch (start us, length us, event | category | flops | bytes accessed | tf_op | source)
XLA Modules:
  0.0 993.1 jit_solution(2038816865999064477)
XLA Ops:
  1.4 496.6 %while.34 = (s32[]{:T(128)}, f32[8,1024]{1,0:T(8,128)S(1)}, f32[128,1024]{1,0:T(8,128)S(1)}, bf16[1024,1024]{1,0:T(8,128)(2,1)}, s32[]{:T(128)}, /*index=5*/f32[...) while((s32[]{:T(128)}, f32[8,1024]{1,0:T(8,128)S(1)}, ...), condition=%wide.region_2.3_spmd, body=%wide.region_0.2_spmd.sunk | while | flops 134389760 | bytes 18383208 | solution.py:55
  3.4 19.7 %all-gather.4 = f32[128,1024]{1,0:T(8,128)S(1)} all-gather(f32[8,1024]{1,0:T(8,128)S(1)} %fusion.48), channel_id=2, replica_groups=mesh['rows'=16,'feat'=16] {'rows'}, dimensions={0}, use_global_device_ids=true | all-gather | bytes 557056 | tf_op jit(solution)/shard_map/while/body/eval_jaxpr/all_gather | solution.py:26
  37.5 15.7 %all-gather.4 = f32[128,1024]{1,0:T(8,128)S(1)} all-gather(f32[8,1024]{1,0:T(8,128)S(1)} %fusion.48), channel_id=2, replica_groups=mesh['rows'=16,'feat'=16] {'rows'}, dimensions={0}, use_global_device_ids=true | all-gather | bytes 557056 | tf_op jit(solution)/shard_map/while/body/eval_jaxpr/all_gather | solution.py:26
  67.5 17.4 %all-gather.4 = f32[128,1024]{1,0:T(8,128)S(1)} all-gather(f32[8,1024]{1,0:T(8,128)S(1)} %fusion.48), channel_id=2, replica_groups=mesh['rows'=16,'feat'=16] {'rows'}, dimensions={0}, use_global_device_ids=true | all-gather | bytes 557056 | tf_op jit(solution)/shard_map/while/body/eval_jaxpr/all_gather | solution.py:26
  99.3 15.7 %all-gather.4 = f32[128,1024]{1,0:T(8,128)S(1)} all-gather(f32[8,1024]{1,0:T(8,128)S(1)} %fusion.48), channel_id=2, replica_groups=mesh['rows'=16,'feat'=16] {'rows'}, dimensions={0}, use_global_device_ids=true | all-gather | bytes 557056 | tf_op jit(solution)/shard_map/while/body/eval_jaxpr/all_gather | solution.py:26
  129.3 17.4 %all-gather.4 = f32[128,1024]{1,0:T(8,128)S(1)} all-gather(f32[8,1024]{1,0:T(8,128)S(1)} %fusion.48), channel_id=2, replica_groups=mesh['rows'=16,'feat'=16] {'rows'}, dimensions={0}, use_global_device_ids=true | all-gather | bytes 557056 | tf_op jit(solution)/shard_map/while/body/eval_jaxpr/all_gather | solution.py:26
  161.0 15.7 %all-gather.4 = f32[128,1024]{1,0:T(8,128)S(1)} all-gather(f32[8,1024]{1,0:T(8,128)S(1)} %fusion.48), channel_id=2, replica_groups=mesh['rows'=16,'feat'=16] {'rows'}, dimensions={0}, use_global_device_ids=true | all-gather | bytes 557056 | tf_op jit(solution)/shard_map/while/body/eval_jaxpr/all_gather | solution.py:26
  191.1 17.4 %all-gather.4 = f32[128,1024]{1,0:T(8,128)S(1)} all-gather(f32[8,1024]{1,0:T(8,128)S(1)} %fusion.48), channel_id=2, replica_groups=mesh['rows'=16,'feat'=16] {'rows'}, dimensions={0}, use_global_device_ids=true | all-gather | bytes 557056 | tf_op jit(solution)/shard_map/while/body/eval_jaxpr/all_gather | solution.py:26
  222.8 15.7 %all-gather.4 = f32[128,1024]{1,0:T(8,128)S(1)} all-gather(f32[8,1024]{1,0:T(8,128)S(1)} %fusion.48), channel_id=2, replica_groups=mesh['rows'=16,'feat'=16] {'rows'}, dimensions={0}, use_global_device_ids=true | all-gather | bytes 557056 | tf_op jit(solution)/shard_map/while/body/eval_jaxpr/all_gather | solution.py:26
  252.9 17.4 %all-gather.4 = f32[128,1024]{1,0:T(8,128)S(1)} all-gather(f32[8,1024]{1,0:T(8,128)S(1)} %fusion.48), channel_id=2, replica_groups=mesh['rows'=16,'feat'=16] {'rows'}, dimensions={0}, use_global_device_ids=true | all-gather | bytes 557056 | tf_op jit(solution)/shard_map/while/body/eval_jaxpr/all_gather | solution.py:26
  284.6 15.7 %all-gather.4 = f32[128,1024]{1,0:T(8,128)S(1)} all-gather(f32[8,1024]{1,0:T(8,128)S(1)} %fusion.48), channel_id=2, replica_groups=mesh['rows'=16,'feat'=16] {'rows'}, dimensions={0}, use_global_device_ids=true | all-gather | bytes 557056 | tf_op jit(solution)/shard_map/while/body/eval_jaxpr/all_gather | solution.py:26
  314.6 17.4 %all-gather.4 = f32[128,1024]{1,0:T(8,128)S(1)} all-gather(f32[8,1024]{1,0:T(8,128)S(1)} %fusion.48), channel_id=2, replica_groups=mesh['rows'=16,'feat'=16] {'rows'}, dimensions={0}, use_global_device_ids=true | all-gather | bytes 557056 | tf_op jit(solution)/shard_map/while/body/eval_jaxpr/all_gather | solution.py:26
  346.4 15.7 %all-gather.4 = f32[128,1024]{1,0:T(8,128)S(1)} all-gather(f32[8,1024]{1,0:T(8,128)S(1)} %fusion.48), channel_id=2, replica_groups=mesh['rows'=16,'feat'=16] {'rows'}, dimensions={0}, use_global_device_ids=true | all-gather | bytes 557056 | tf_op jit(solution)/shard_map/while/body/eval_jaxpr/all_gather | solution.py:26
  376.4 17.4 %all-gather.4 = f32[128,1024]{1,0:T(8,128)S(1)} all-gather(f32[8,1024]{1,0:T(8,128)S(1)} %fusion.48), channel_id=2, replica_groups=mesh['rows'=16,'feat'=16] {'rows'}, dimensions={0}, use_global_device_ids=true | all-gather | bytes 557056 | tf_op jit(solution)/shard_map/while/body/eval_jaxpr/all_gather | solution.py:26
  438.2 17.4 %all-gather.4 = f32[128,1024]{1,0:T(8,128)S(1)} all-gather(f32[8,1024]{1,0:T(8,128)S(1)} %fusion.48), channel_id=2, replica_groups=mesh['rows'=16,'feat'=16] {'rows'}, dimensions={0}, use_global_device_ids=true | all-gather | bytes 557056 | tf_op jit(solution)/shard_map/while/body/eval_jaxpr/all_gather | solution.py:26
  498.0 494.3 %while.35 = (s32[]{:T(128)}, f32[8,1024]{1,0:T(8,128)S(1)}, f32[128,1024]{1,0:T(8,128)S(1)}, bf16[1024,1024]{1,0:T(8,128)(2,1)}, s32[]{:T(128)}, /*index=5*/f32[...) while((s32[]{:T(128)}, f32[8,1024]{1,0:T(8,128)S(1)}, ...), condition=%wide.region_5.6_spmd, body=%wide.region_3.5_spmd.sunk | while | flops 134389760 | bytes 18383220 | solution.py:55
  500.0 17.4 %all-gather.5 = f32[128,1024]{1,0:T(8,128)S(1)} all-gather(f32[8,1024]{1,0:T(8,128)S(1)} %fusion.56), channel_id=3, replica_groups=mesh['rows'=16,'feat'=16] {'rows'}, dimensions={0}, use_global_device_ids=true | all-gather | bytes 557056 | tf_op jit(solution)/shard_map/while/body/eval_jaxpr/all_gather | solution.py:26
  561.8 17.4 %all-gather.5 = f32[128,1024]{1,0:T(8,128)S(1)} all-gather(f32[8,1024]{1,0:T(8,128)S(1)} %fusion.56), channel_id=3, replica_groups=mesh['rows'=16,'feat'=16] {'rows'}, dimensions={0}, use_global_device_ids=true | all-gather | bytes 557056 | tf_op jit(solution)/shard_map/while/body/eval_jaxpr/all_gather | solution.py:26
  623.6 17.4 %all-gather.5 = f32[128,1024]{1,0:T(8,128)S(1)} all-gather(f32[8,1024]{1,0:T(8,128)S(1)} %fusion.56), channel_id=3, replica_groups=mesh['rows'=16,'feat'=16] {'rows'}, dimensions={0}, use_global_device_ids=true | all-gather | bytes 557056 | tf_op jit(solution)/shard_map/while/body/eval_jaxpr/all_gather | solution.py:26
  685.3 17.4 %all-gather.5 = f32[128,1024]{1,0:T(8,128)S(1)} all-gather(f32[8,1024]{1,0:T(8,128)S(1)} %fusion.56), channel_id=3, replica_groups=mesh['rows'=16,'feat'=16] {'rows'}, dimensions={0}, use_global_device_ids=true | all-gather | bytes 557056 | tf_op jit(solution)/shard_map/while/body/eval_jaxpr/all_gather | solution.py:26
  747.1 17.4 %all-gather.5 = f32[128,1024]{1,0:T(8,128)S(1)} all-gather(f32[8,1024]{1,0:T(8,128)S(1)} %fusion.56), channel_id=3, replica_groups=mesh['rows'=16,'feat'=16] {'rows'}, dimensions={0}, use_global_device_ids=true | all-gather | bytes 557056 | tf_op jit(solution)/shard_map/while/body/eval_jaxpr/all_gather | solution.py:26
  808.9 17.4 %all-gather.5 = f32[128,1024]{1,0:T(8,128)S(1)} all-gather(f32[8,1024]{1,0:T(8,128)S(1)} %fusion.56), channel_id=3, replica_groups=mesh['rows'=16,'feat'=16] {'rows'}, dimensions={0}, use_global_device_ids=true | all-gather | bytes 557056 | tf_op jit(solution)/shard_map/while/body/eval_jaxpr/all_gather | solution.py:26
  870.7 17.4 %all-gather.5 = f32[128,1024]{1,0:T(8,128)S(1)} all-gather(f32[8,1024]{1,0:T(8,128)S(1)} %fusion.56), channel_id=3, replica_groups=mesh['rows'=16,'feat'=16] {'rows'}, dimensions={0}, use_global_device_ids=true | all-gather | bytes 557056 | tf_op jit(solution)/shard_map/while/body/eval_jaxpr/all_gather | solution.py:26
  932.5 17.4 %all-gather.5 = f32[128,1024]{1,0:T(8,128)S(1)} all-gather(f32[8,1024]{1,0:T(8,128)S(1)} %fusion.56), channel_id=3, replica_groups=mesh['rows'=16,'feat'=16] {'rows'}, dimensions={0}, use_global_device_ids=true | all-gather | bytes 557056 | tf_op jit(solution)/shard_map/while/body/eval_jaxpr/all_gather | solution.py:26
  (303 shorter events, 616.6 us)
Async XLA Ops:
  28.2 7.3 collective-permute-start
  58.3 7.3 collective-permute-start
  90.0 7.3 collective-permute-start
  120.1 7.3 collective-permute-start
  151.8 7.3 collective-permute-start
  181.9 7.3 collective-permute-start
  213.6 7.3 collective-permute-start
  243.6 7.3 collective-permute-start
  275.4 7.3 collective-permute-start
  305.4 7.3 collective-permute-start
  337.2 7.3 collective-permute-start
  367.2 7.3 collective-permute-start
  398.9 7.3 collective-permute-start
  429.0 7.3 collective-permute-start
  460.7 7.3 collective-permute-start
  490.8 7.3 collective-permute-start
  522.5 7.3 collective-permute-start.1
  552.6 7.3 collective-permute-start.1
  614.3 7.3 collective-permute-start.1
  676.1 7.3 collective-permute-start.1
  737.9 7.3 collective-permute-start.1
  799.7 7.3 collective-permute-start.1
  893.2 7.3 collective-permute-start.1
  955.0 7.3 collective-permute-start.1
  (41 other events, 200.7 us)
